TPU v7x, 128 devices: a whole 4x4x4 slice. The times are simulated.
128 devices in a mesh: doc: 8 (over x, core), term: 16 (over z, y).
Axes of the slice: x: 4, y: 4, z: 4, core: 2. Of those that a mesh axis runs over, the one named last changes fastest.
Arguments:
- query_states: bfloat16 [512, 32, 768], P('doc'), may hold values from -6 to 6
- token_ids: int32 [512, 32], P('doc'), may hold values from 0 to 30521, as said below
- transform_weight: bfloat16 [768, 768], replicated, may hold values from -0.21875 to 0.21875
- transform_bias: float32 [768], replicated, may hold values from -3 to 3
- norm_gain: float32 [768], replicated, may hold values from 0.5 to 1.5
- norm_bias: float32 [768], replicated, may hold values from -3 to 3
- decoder_weight: bfloat16 [768, 30720], P(None, 'term'), may hold values from -0.21875 to 0.21875
- decoder_bias: float32 [30720], P('term'), may hold values from -2.5 to 0.5
- candidates: int32 [512, 32], P('doc'), may hold values from 0 to 127, all different within a row; in each aligned block of 64 rows (0 to 63, 64 to 127, ...) at most 32 rows name the same one
- occupancy: int32 [128, 240], P('doc', 'term'), may hold values 0 or 1
- doc_blocks: bfloat16 [128, 240, 128, 128], P('doc', 'term'), may hold values from -0.046875 to 0.046875
Outputs:
- query_weights: bfloat16 [512, 30720], P('doc', 'term')
- scores: float32 [512, 32, 128], P('doc', None, 'term')
Inputs may be any that keep to these rules, and one draw needn't show every extreme that they name: `token_ids`: id 0 marks padding: a query has non-zero ids at its first positions, at least 8 of them, and 0 after them. `candidates`: A query names 32 different tiles; among the 64 queries of one doc index no tile is named by more than 32 of them.
All inputs are finite; a program needn't handle non-finite values. No bound on the sum of `occupancy` on one device may be relied on, other than what follows from the above.
Results may differ from a plain program's by a relative error of at most 0.0041.
Values may be sent and summed in bfloat16 or wider, within the bound.
A program may use at most 128 MiB of HBM per device.

v0:
```python
import jax
import jax.numpy as jnp
from jax import lax
from jax.sharding import PartitionSpec as P

VOCAB = 30522
MOST = 32


def tile_ranks(cand_rows, tile_total):
    tile_index = lax.iota(jnp.int32, tile_total)
    tile_hits = jnp.sum((cand_rows[..., None] == tile_index).astype(jnp.int32), axis=-2)
    tile_before = jnp.cumsum(tile_hits, axis=-2) - tile_hits
    return (tile_hits, tile_before)


def slot_sources(hits_by_tile, before_by_tile, capacity):
    row_total = hits_by_tile.shape[-1]
    slot_index = lax.iota(jnp.int32, capacity)
    chosen = (hits_by_tile[..., None, :] > 0) & (
        before_by_tile[..., None, :] == slot_index[:, None]
    )
    source_row = jnp.sum(jnp.where(chosen, lax.iota(jnp.int32, row_total), 0), axis=-1)
    return (source_row, jnp.any(chosen, axis=-1))


def body(
    query_states,
    token_ids,
    transform_weight,
    transform_bias,
    norm_gain,
    norm_bias,
    decoder_weight,
    decoder_bias,
    candidates,
    occupancy,
    doc_blocks,
):
    query_count, query_length, model_width = query_states.shape
    vocab_local = decoder_weight.shape[1]
    tile_local, blocks_local, tile_docs, block_terms = doc_blocks.shape
    cand_count = candidates.shape[1]
    term_index = lax.axis_index("term")
    doc_index = lax.axis_index("doc")
    doc_count = lax.axis_size("doc")
    term_count = lax.axis_size("term")
    tile_total = doc_count * tile_local
    hidden = (
        jnp.dot(
            query_states.reshape(query_count * query_length, model_width),
            transform_weight,
            preferred_element_type=jnp.float32,
        )
        + transform_bias
    )
    hidden = jax.nn.gelu(hidden, approximate=False)
    centred = hidden - jnp.mean(hidden, axis=-1, keepdims=True)
    spread = jnp.mean(centred * centred, axis=-1, keepdims=True)
    normed = (centred * lax.rsqrt(spread + 1e-06) * norm_gain + norm_bias).astype(jnp.bfloat16)
    logits = jnp.dot(normed, decoder_weight, preferred_element_type=jnp.float32) + decoder_bias
    activated = jnp.log1p(jnp.maximum(logits, 0.0)).reshape(query_count, query_length, vocab_local)
    live_mask = (token_ids != 0).astype(jnp.float32)[:, :, None]
    columns = term_index * vocab_local + lax.iota(jnp.int32, vocab_local)
    vocab_keep = (columns < VOCAB).astype(jnp.float32)
    weights = (jnp.max(activated * live_mask, axis=1) * vocab_keep).astype(jnp.bfloat16)
    own_hits, own_before = tile_ranks(candidates, tile_total)
    all_weights, all_cand = (
        lax.all_gather(weights, "doc", axis=0, tiled=True),
        lax.all_gather(candidates, "doc", axis=0, tiled=True),
    )
    local_cand = (all_cand - doc_index * tile_local).reshape(doc_count, query_count, cand_count)
    tile_hits, tile_before = tile_ranks(local_cand, tile_local)
    source_row, slot_valid = slot_sources(
        jnp.swapaxes(tile_hits, 1, 2), jnp.swapaxes(tile_before, 1, 2), MOST
    )
    flat_index = lax.iota(jnp.int32, doc_count)[:, None, None] * query_count + source_row
    buffer = jnp.take(all_weights, flat_index.reshape(-1), axis=0).reshape(
        doc_count, tile_local, MOST, vocab_local
    )
    buffer = buffer * slot_valid.astype(jnp.bfloat16)[..., None]
    occupied = occupancy.astype(jnp.bfloat16)
    masked = (
        buffer.reshape(doc_count, tile_local, MOST, blocks_local, block_terms)
        * occupied[None, :, None, :, None]
    )
    partial_value = jnp.einsum(
        "jtrbc,tbdc->jtrd", masked, doc_blocks, preferred_element_type=jnp.float32
    )
    slice_width = tile_docs // term_count
    score_total = lax.psum(partial_value, "term")
    score_share = lax.dynamic_slice_in_dim(score_total, term_index * slice_width, slice_width, 3)
    returned = lax.all_to_all(score_share, "doc", split_axis=0, concat_axis=1, tiled=True)
    slot_rank = jnp.take_along_axis(own_before, candidates, axis=1)
    flat_index = candidates * MOST + slot_rank
    scores = jnp.take(returned.reshape(-1, slice_width), flat_index.reshape(-1), axis=0)
    scores = scores.reshape(query_count, cand_count, slice_width)
    return (weights, scores)


def solution(mesh):
    placed = (
        P("doc", None, None),
        P("doc", None),
        P(),
        P(),
        P(),
        P(),
        P(None, "term"),
        P("term"),
        P("doc", None),
        P("doc", "term"),
        P("doc", "term", None, None),
    )
    return jax.shard_map(
        body,
        mesh=mesh,
        in_specs=placed,
        out_specs=(P("doc", "term"), P("doc", None, "term")),
        check_vma=False,
    )
```

profile of v0, /device:TPU:1, one launch (start us, length us, event | category | flops | bytes accessed | tf_op | source)
XLA Modules:
  0.0 286.4 jit_solution(9171432627118115750)
XLA Ops:
  7.2 0.9 copy.49
  9.1 17.5 %fusion.25 = (f32[2048]{0:T(1024)S(1)}, f32[2048,768]{0,1:T(8,128)S(1)}) fusion(f32[768]{0:T(1024)} %param.14, bf16[2048,768]{1,0:T(8,128)(2,1)S(1)} %bitcast.34, bf16[768,768]{1,0:T(8,128)(2,1)} %param.13), kind=kOutput, calls=%fused_computation.67 | convolution fusion | flops 2519726080 | bytes 10628096 | tf_op jit(solution)/shard_map/dot_general | solution.py:50
  27.4 1.1 copy-done.4
  28.5 13.7 %multiply_reduce_fusion = f32[64,1920]{1,0:T(8,128)S(1)} fusion(f32[64,32]{1,0:T(8,128)S(1)} %compare_convert_fusion, f32[1920]{0:T(1024)S(1)} %copy-done.5, bf16[768,1920]{1,0:T(8,128)(2,1)S(1)} %copy-done.4, f32[2048,768]{0,1:T(8,128)S(1)} %get-tuple-element.7, f32[768]{0:T(1024)S(1)} %copy-done.6, f32[768]{0:T(1024)S(1)} %copy-done.7, ...), kind=kOutput, calls=%fused_computation.6 | convolution fusion | flops 6063267840 | bytes 9770496 | tf_op jit(solution)/shard_map/dot_general | solution.py:61
  43.0 14.4 %all-gather = s32[8,64,32]{1,2,0:T(8,128)S(1)} all-gather(s32[1,64,32]{1,2,0:T(8,128)S(1)} %bitcast.39), channel_id=1, replica_groups=mesh['doc'=8,'term'=16] {'doc'}, dimensions={0}, use_global_device_ids=true | all-gather | bytes 73728 | tf_op jit(solution)/shard_map/all_gather | solution.py:70
  57.9 6.6 %fusion.23 = s32[8,16,64]{1,0,2:T(8,128)S(1)} fusion(s32[8,64,16]{2,0,1:T(8,128)S(1)} %copy.56), kind=kOutput, calls=%fused_computation.43 | output fusion | flops 524288 | bytes 65536 | tf_op jit(solution)/shard_map/jit(cumsum)/reduce_window_sum | solution.py:13
  64.6 2.2 select_reduce_fusion
  67.1 2.3 fusion.17
  69.4 2.2 all-gather.3.cloned.1.call-done
  71.6 31.8 %gather_fusion = bf16[4096,1920]{1,0:T(8,128)(2,1)} fusion(bf16[512,1920]{1,0:T(8,128)(2,1)} %all-gather.3.cloned.1.call-done, s32[4096]{0:T(1024)S(1)} %broadcast_clamp_fusion), kind=kCustom, calls=%fused_computation | custom fusion | bytes 31473664 | tf_op jit(solution)/shard_map/jit(_take)/gather | solution.py:78
  103.4 27.2 %gather.18 = bf16[8,16,32,15,128]{4,3,2,1,0:T(8,128)(2,1)} reshape(bf16[4096,1920]{1,0:T(8,128)(2,1)} %gather_fusion) | data formatting | bytes 31457280 | tf_op jit(solution)/shard_map/jit(_take)/gather | solution.py:78
  130.6 14.0 %multiply_multiply_fusion = bf16[8,16,32,15,128]{4,3,2,1,0:T(8,128)(2,1)} fusion(bf16[8,16,32,15,128]{4,3,2,1,0:T(8,128)(2,1)} %gather.18, pred[8,16,32]{2,1,0:T(8,128)(4,1)S(1)} %get-tuple-element.4, bf16[16,15]{1,0:T(8,128)(2,1)S(1)} %convert_element_type.39, bf16[8,16,32]{2,1,0:T(8,128)(2,1)S(1)} %convert_element_type.38), kind=kLoop, calls=%fused_computation.3 | loop fusion | flops 23592960 | bytes 31470048 | tf_op jit(solution)/shard_map/mul | solution.py:84
  144.6 13.5 %fusion.18 = f32[8,16,32,128]{3,2,0,1:T(8,128)} fusion(bf16[16,15,128,128]{3,2,1,0:T(8,128)(2,1)} %param.21, bf16[8,16,32,15,128]{4,3,2,1,0:T(8,128)(2,1)} %multiply_multiply_fusion), kind=kOutput, calls=%fused_computation.39 | convolution fusion | flops 2013265920 | bytes 25690112 | tf_op jit(solution)/shard_map/jtrbc,tbdc->jtrd/dot_general | solution.py:87
  158.8 13.1 %gather_fusion.2 = s32[2048]{0:T(1024)S(1)} fusion(s32[64,128]{1,0:T(8,128)S(1)} %sub.26, s32[2048]{0:T(1024)S(1)} %reshape.174), kind=kCustom, calls=%fused_computation.2 | custom fusion | bytes 32768 | tf_op jit(solution)/shard_map/jit(take_along_axis)/gather | solution.py:94
  172.1 75.3 %all-reduce.2.cloned.1.call-done = f32[8,16,32,128]{3,2,0,1:T(8,128)} async-done(((f32[8,16,32,128]{3,2,0,1:T(8,128)}), f32[8,16,32,128]{3,2,0,1:T(8,128)}) %all-reduce.2.cloned.1.call-update) | async-done | bytes 2097168 | tf_op jit(solution)/shard_map/psum | solution.py:91
  247.4 2.2 constant_dynamic-slice_fusion
  250.2 0.9 reshape.192
  251.1 6.0 %all-to-all-start = ((f32[8,1,4096]{2,1,0:T(1,128)}), f32[8,1,4096]{2,1,0:T(1,128)S(1)}, u32[]{:S(2)}, u32[]{:S(2)}) async-start(f32[8,1,4096]{2,1,0:T(1,128)} %reshape.192), calls=%async_computation | async-start | bytes 262144 | tf_op jit(solution)/shard_map/all_to_all | solution.py:93
  257.1 5.3 %all-to-all-done = f32[8,1,4096]{2,1,0:T(1,128)S(1)} async-done(((f32[8,1,4096]{2,1,0:T(1,128)}), f32[8,1,4096]{2,1,0:T(1,128)S(1)}, u32[]{:S(2)}, u32[]{:S(2)}) %all-to-all-start) | async-done | bytes 131104 | tf_op jit(solution)/shard_map/all_to_all | solution.py:93
  262.9 1.0 reduce
  263.8 1.0 reshape.193
  264.8 3.2 %copy.66 = f32[8,16,32,8]{3,2,1,0:T(8,128)} copy(f32[8,16,32,8]{2,3,1,0:T(8,128)} %bitcast.38) | data formatting | bytes 262144 | tf_op jit(solution)/shard_map/reshape | solution.py:96
  268.0 9.1 %gather_fusion.1 = f32[2048,8]{1,0:T(8,128)} fusion(f32[4096,8]{1,0:T(8,128)} %bitcast.35, s32[2048]{0:T(1024)S(1)} %broadcast_clamp_fusion.1), kind=kCustom, calls=%fused_computation.1 | custom fusion | bytes 139264 | tf_op jit(solution)/shard_map/jit(_take)/gather | solution.py:96
  277.1 1.8 copy.63
  (52 shorter events, 6.0 us)
Async XLA Ops:
  7.2 1.9 copy-start
  7.2 64.4 %all-gather.3.cloned.1.call-start = ((), (), s32[]{:S(2)}) async-start(), calls=%async_computation.1 | async-start | bytes 2211840 | tf_op jit(solution)/shard_map/all_gather | solution.py:69
  26.6 1.8 copy-start.4
  26.6 1.8 copy-start.5
  26.6 1.8 copy-start.6
  26.6 1.8 copy-start.7
  28.4 14.5 %copy-start.3 = (s32[16,15]{1,0:T(8,128)S(1)}, s32[16,15]{1,0:T(8,128)}, u32[]{:S(2)}) copy-start(s32[16,15]{1,0:T(8,128)} %param.20) | copy-start | bytes 2884
  28.4 14.6 %copy-start.2 = (s32[64,32]{0,1:T(8,128)S(1)}, s32[64,32]{0,1:T(8,128)}, u32[]{:S(2)}) copy-start(s32[64,32]{0,1:T(8,128)} %param.19) | copy-start | bytes 24580
  42.9 204.5 %all-reduce.2.cloned.1.call-start = ((), (), s32[]{:S(2)}) async-start(), calls=%async_computation.2 | async-start | bytes 4194304 | tf_op jit(solution)/shard_map/psum | solution.py:91
  251.1 11.2 %all-to-all-start = ((f32[8,1,4096]{2,1,0:T(1,128)}), f32[8,1,4096]{2,1,0:T(1,128)S(1)}, u32[]{:S(2)}, u32[]{:S(2)}) async-start(f32[8,1,4096]{2,1,0:T(1,128)} %reshape.192), calls=%async_computation | async-start | bytes 262144 | tf_op jit(solution)/shard_map/all_to_all | solution.py:93
  264.8 14.8 %copy-start.1 = (bf16[64,32,768]{2,1,0:T(8,128)(2,1)S(1)}, bf16[64,32,768]{2,1,0:T(8,128)(2,1)}, u32[]{:S(2)}) copy-start(bf16[64,32,768]{2,1,0:T(8,128)(2,1)} %param.11) | copy-start | bytes 9437188
Sparse Core Ops, SparseCore 0:
  43.0 28.5 all-gather.2
  158.2 89.1 all-reduce.1
where the time goes:
time: 288 us; the launch traced here: 286 us
  local copies, waits for them, and re-layouts  95 us (33%)
  waiting for transfers between devices  82.8 us (29%)
  matrix products  44.7 us (16%)
  other arithmetic  29.1 us (10%)
  blocking collectives  14.4 us (5%)
  between operations  14.3 us (5%)
  starting transfers between devices  6.05 us (2%)
    psum x1, waiting for transfers between devices, body(): score_total = lax.psum(partial_value, 'term')  75.3 us
    gather x2, local copies, waits for them, and re-layouts, body(): jnp.take(all_weights, flat_index.reshape(-1), axis=0)  59 us
    dot_general x1, matrix products, body(): jnp.dot(query_states.reshape(query_count * query_length, model_width), tr...  17.5 us
    all_gather x1, blocking collectives, body(): lax.all_gather(candidates, 'doc', axis=0, tiled=True)  14.4 us
    mul x1, other arithmetic, body(): buffer.reshape(doc_count, tile_local, MOST, blocks_local, block_terms)  14 us
    dot_general x1, matrix products, body(): jnp.dot(normed, decoder_weight, preferred_element_type=jnp.float32)  13.7 us
    dot_general x1, matrix products, body(): jnp.einsum('jtrbc,tbdc->jtrd', masked, doc_blocks, preferred_element_type...  13.5 us
    gather x3, local copies, waits for them, and re-layouts, body(): slot_rank = jnp.take_along_axis(own_before, candidates, axis=1)  13.2 us
  transfers between devices with their start and end apart: 3, of which 3 were waited for; matrix products, arithmetic and copies ran while one was open for 9% of the time, Pallas kernels for 0%

commit v1 on v0

--- a/solution.py
+++ b/solution.py
@@ -88,7 +88,23 @@
         "jtrbc,tbdc->jtrd", masked, doc_blocks, preferred_element_type=jnp.float32
     )
     slice_width = tile_docs // term_count
-    score_total = lax.psum(partial_value, "term")
+
+    def forms_move(inp):
+        link_axis = "term"
+        amount_of = lax.axis_size(link_axis)
+
+        def _unite_frame(shaped, y2):
+            if y2 >= amount_of:
+                return shaped
+            known = range(amount_of)
+            met_up = map(lambda to_i: (to_i, to_i ^ y2), known)
+            return _unite_frame(
+                shaped + lax.ppermute(shaped, axis_name=link_axis, perm=list(met_up)), 2 * y2
+            )
+
+        return _unite_frame(inp, 1)
+
+    score_total = forms_move(partial_value)
     score_share = lax.dynamic_slice_in_dim(score_total, term_index * slice_width, slice_width, 3)
     returned = lax.all_to_all(score_share, "doc", split_axis=0, concat_axis=1, tiled=True)
     slot_rank = jnp.take_along_axis(own_before, candidates, axis=1)

time: 288 us -> 390 us (1.35)
  waiting for transfers between devices: 82.8 us -> 171 us
  starting transfers between devices: 6.05 us -> 15.8 us
  other arithmetic: 29.1 us -> 34.6 us
    ppermute x0 -> x4, waiting for transfers between devices: none -> 163 us  [_unite_frame(): lax.ppermute(shaped, axis_name=link_axis, perm=list(met_up))]
    psum x1 -> x0, waiting for transfers between devices: 75.3 us -> none  [body(): score_total = lax.psum(partial_value, 'term')]
    ppermute x0 -> x4, starting transfers between devices: none -> 8.66 us  [_unite_frame(): lax.ppermute(shaped, axis_name=link_axis, perm=list(met_up))]
    add x0 -> x4, other arithmetic: none -> 5.53 us  [_unite_frame(): shaped + lax.ppermute(shaped, axis_name=link_axis, perm=list(met_up))]
  transfers between devices with their start and end apart: 3 -> 6, of which waited for: 3 -> 6; matrix products, arithmetic and copies ran while one was open for 9% -> 7% of each run, Pallas kernels for 0% -> 0%
where the time goes in v1:
time: 390 us; the launch traced here: 388 us
  waiting for transfers between devices  171 us (44%)
  local copies, waits for them, and re-layouts  94.4 us (24%)
  matrix products  43.9 us (11%)
  other arithmetic  34.6 us (9%)
  starting transfers between devices  15.8 us (4%)
  blocking collectives  14.4 us (4%)
  between operations  14.3 us (4%)
    ppermute x4, waiting for transfers between devices, _unite_frame(): lax.ppermute(shaped, axis_name=link_axis, perm=list(met_up))  163 us
    gather x2, local copies, waits for them, and re-layouts, body(): jnp.take(all_weights, flat_index.reshape(-1), axis=0)  59 us
    dot_general x1, matrix products, body(): jnp.dot(query_states.reshape(query_count * query_length, model_width), tr...  17.5 us
    all_gather x1, blocking collectives, body(): lax.all_gather(candidates, 'doc', axis=0, tiled=True)  14.4 us
    mul x1, other arithmetic, body(): buffer.reshape(doc_count, tile_local, MOST, blocks_local, block_terms)  14 us
    dot_general x1, matrix products, body(): jnp.dot(normed, decoder_weight, preferred_element_type=jnp.float32)  13.7 us
    gather x3, local copies, waits for them, and re-layouts, body(): slot_rank = jnp.take_along_axis(own_before, candidates, axis=1)  13.2 us
    dot_general x1, matrix products, body(): jnp.einsum('jtrbc,tbdc->jtrd', masked, doc_blocks, preferred_element_type...  12.7 us
  transfers between devices with their start and end apart: 6, of which 6 were waited for; matrix products, arithmetic and copies ran while one was open for 7% of the time, Pallas kernels for 0%

profile of v1, /device:TPU:1, one launch (start us, length us, event | category | flops | bytes accessed | tf_op | source)
XLA Modules:
  0.0 388.4 jit_solution(14077223139723578866)
XLA Ops:
  9.1 17.5 %fusion.25 = (f32[2048]{0:T(1024)S(1)}, f32[2048,768]{0,1:T(8,128)S(1)}) fusion(f32[768]{0:T(1024)} %param.14, bf16[2048,768]{1,0:T(8,128)(2,1)S(1)} %bitcast.34, bf16[768,768]{1,0:T(8,128)(2,1)} %param.13), kind=kOutput, calls=%fused_computation.67 | convolution fusion | flops 2519726080 | bytes 10628096 | tf_op jit(solution)/shard_map/dot_general | solution.py:50
  28.5 13.7 %multiply_reduce_fusion = f32[64,1920]{1,0:T(8,128)S(1)} fusion(f32[64,32]{1,0:T(8,128)S(1)} %compare_convert_fusion, f32[1920]{0:T(1024)S(1)} %copy-done.5, bf16[768,1920]{1,0:T(8,128)(2,1)S(1)} %copy-done.4, f32[2048,768]{0,1:T(8,128)S(1)} %get-tuple-element.7, f32[768]{0:T(1024)S(1)} %copy-done.6, f32[768]{0:T(1024)S(1)} %copy-done.7, ...), kind=kOutput, calls=%fused_computation.6 | convolution fusion | flops 6063267840 | bytes 9770496 | tf_op jit(solution)/shard_map/dot_general | solution.py:61
  43.0 14.4 %all-gather = s32[8,64,32]{1,2,0:T(8,128)S(1)} all-gather(s32[1,64,32]{1,2,0:T(8,128)S(1)} %bitcast.39), channel_id=1, replica_groups=mesh['doc'=8,'term'=16] {'doc'}, dimensions={0}, use_global_device_ids=true | all-gather | bytes 73728 | tf_op jit(solution)/shard_map/all_gather | solution.py:70
  57.8 6.6 %fusion.23 = s32[8,16,64]{1,0,2:T(8,128)S(1)} fusion(s32[8,64,16]{2,0,1:T(8,128)S(1)} %copy.56), kind=kOutput, calls=%fused_computation.44 | output fusion | flops 524288 | bytes 65536 | tf_op jit(solution)/shard_map/jit(cumsum)/reduce_window_sum | solution.py:13
  64.6 2.2 select_reduce_fusion
  67.0 2.3 fusion.17
  69.4 2.3 all-gather.3.cloned.1.call-done
  71.6 31.8 %gather_fusion = bf16[4096,1920]{1,0:T(8,128)(2,1)} fusion(bf16[512,1920]{1,0:T(8,128)(2,1)} %all-gather.3.cloned.1.call-done, s32[4096]{0:T(1024)S(1)} %broadcast_clamp_fusion), kind=kCustom, calls=%fused_computation | custom fusion | bytes 31473664 | tf_op jit(solution)/shard_map/jit(_take)/gather | solution.py:78
  103.5 27.2 %gather.18 = bf16[8,16,32,15,128]{4,3,2,1,0:T(8,128)(2,1)} reshape(bf16[4096,1920]{1,0:T(8,128)(2,1)} %gather_fusion) | data formatting | bytes 31457280 | tf_op jit(solution)/shard_map/jit(_take)/gather | solution.py:78
  130.6 14.0 %multiply_multiply_fusion = bf16[8,16,32,15,128]{4,3,2,1,0:T(8,128)(2,1)} fusion(bf16[8,16,32,15,128]{4,3,2,1,0:T(8,128)(2,1)} %gather.18, pred[8,16,32]{2,1,0:T(8,128)(4,1)S(1)} %get-tuple-element.4, bf16[16,15]{1,0:T(8,128)(2,1)S(1)} %convert_element_type.39, bf16[8,16,32]{2,1,0:T(8,128)(2,1)S(1)} %convert_element_type.38), kind=kLoop, calls=%fused_computation.3 | loop fusion | flops 23592960 | bytes 31470048 | tf_op jit(solution)/shard_map/mul | solution.py:84
  144.6 12.7 %fusion.18 = f32[8,16,32,128]{3,2,0,1:T(8,128)S(1)} fusion(bf16[16,15,128,128]{3,2,1,0:T(8,128)(2,1)} %param.21, bf16[8,16,32,15,128]{4,3,2,1,0:T(8,128)(2,1)} %multiply_multiply_fusion), kind=kOutput, calls=%fused_computation.40 | convolution fusion | flops 2013265920 | bytes 25690112 | tf_op jit(solution)/shard_map/jtrbc,tbdc->jtrd/dot_general | solution.py:87
  158.5 45.8 %collective-permute-done = f32[8,16,32,128]{3,2,0,1:T(8,128)S(1)} collective-permute-done((f32[8,16,32,128]{3,2,0,1:T(8,128)S(1)}, f32[8,16,32,128]{3,2,0,1:T(8,128)S(1)}, u32[]{:S(2)}, u32[]{:S(2)}) %collective-permute-start) | collective-permute-done | bytes 2097184 | tf_op jit(solution)/shard_map/ppermute | solution.py:102
  204.8 2.8 collective-permute-start.1
  207.6 44.8 %collective-permute-done.1 = f32[8,16,32,128]{3,2,0,1:T(8,128)S(1)} collective-permute-done((f32[8,16,32,128]{3,2,0,1:T(8,128)S(1)}, f32[8,16,32,128]{3,2,0,1:T(8,128)S(1)}, u32[]{:S(2)}, u32[]{:S(2)}) %collective-permute-start.1) | collective-permute-done | bytes 2097184 | tf_op jit(solution)/shard_map/ppermute | solution.py:102
  254.3 43.9 %collective-permute-done.2 = f32[8,16,32,128]{3,2,0,1:T(8,128)S(1)} collective-permute-done((f32[8,16,32,128]{3,2,0,1:T(8,128)S(1)}, f32[8,16,32,128]{3,2,0,1:T(8,128)S(1)}, u32[]{:S(2)}, u32[]{:S(2)}) %collective-permute-start.2) | collective-permute-done | bytes 2097184 | tf_op jit(solution)/shard_map/ppermute | solution.py:102
  298.7 3.2 collective-permute-start.3
  302.6 13.1 %gather_fusion.2 = s32[2048]{0:T(1024)S(1)} fusion(s32[64,128]{1,0:T(8,128)S(1)} %sub.26, s32[2048]{0:T(1024)S(1)} %reshape.174), kind=kCustom, calls=%fused_computation.2 | custom fusion | bytes 32768 | tf_op jit(solution)/shard_map/jit(take_along_axis)/gather | solution.py:110
  315.9 28.9 %collective-permute-done.3 = f32[8,16,32,128]{3,2,0,1:T(8,128)} collective-permute-done((f32[8,16,32,128]{3,2,0,1:T(8,128)S(1)}, f32[8,16,32,128]{3,2,0,1:T(8,128)}, u32[]{:S(2)}, u32[]{:S(2)}) %collective-permute-start.3) | collective-permute-done | bytes 2097184 | tf_op jit(solution)/shard_map/ppermute | solution.py:102
  344.8 4.0 %dynamic-slice_add_fusion = f32[8,16,32,8]{3,2,0,1:T(8,128)} fusion(f32[8,16,32,128]{3,2,0,1:T(8,128)} %collective-permute-done.3, s32[]{:T(128)S(6)} %select_n.67, f32[8,16,32,128]{3,2,0,1:T(8,128)S(1)} %add.161), kind=kLoop, calls=%fused_computation.33 | loop fusion | flops 32768 | bytes 393220 | tf_op jit(solution)/shard_map/add | solution.py:102
  348.9 2.2 copy.60
  352.0 7.1 %all-to-all-start = ((f32[8,1,4096]{2,1,0:T(1,128)}), f32[8,1,4096]{2,1,0:T(1,128)S(1)}, u32[]{:S(2)}, u32[]{:S(2)}) async-start(f32[8,1,4096]{2,1,0:T(1,128)} %reshape.192), calls=%async_computation | async-start | bytes 262144 | tf_op jit(solution)/shard_map/all_to_all | solution.py:109
  359.1 5.3 %all-to-all-done = f32[8,1,4096]{2,1,0:T(1,128)S(1)} async-done(((f32[8,1,4096]{2,1,0:T(1,128)}), f32[8,1,4096]{2,1,0:T(1,128)S(1)}, u32[]{:S(2)}, u32[]{:S(2)}) %all-to-all-start) | async-done | bytes 131104 | tf_op jit(solution)/shard_map/all_to_all | solution.py:109
  366.8 3.2 copy.66
  370.0 9.1 %gather_fusion.1 = f32[2048,8]{1,0:T(8,128)} fusion(f32[4096,8]{1,0:T(8,128)} %bitcast.35, s32[2048]{0:T(1024)S(1)} %broadcast_clamp_fusion.1), kind=kCustom, calls=%fused_computation.1 | custom fusion | bytes 139264 | tf_op jit(solution)/shard_map/jit(_take)/gather | solution.py:112
  (60 shorter events, 16.1 us)
Async XLA Ops:
  7.2 1.9 copy-start
  7.2 64.4 %all-gather.3.cloned.1.call-start = ((), (), s32[]{:S(2)}) async-start(), calls=%async_computation.1 | async-start | bytes 2211840 | tf_op jit(solution)/shard_map/all_gather | solution.py:69
  26.6 1.8 copy-start.4
  26.6 1.8 copy-start.5
  26.6 1.8 copy-start.6
  26.6 1.8 copy-start.7
  28.4 14.5 %copy-start.3 = (s32[16,15]{1,0:T(8,128)S(1)}, s32[16,15]{1,0:T(8,128)}, u32[]{:S(2)}) copy-start(s32[16,15]{1,0:T(8,128)} %param.20) | copy-start | bytes 2884
  28.4 14.5 %copy-start.2 = (s32[64,32]{0,1:T(8,128)S(1)}, s32[64,32]{0,1:T(8,128)}, u32[]{:S(2)}) copy-start(s32[64,32]{0,1:T(8,128)} %param.19) | copy-start | bytes 24580
  157.2 47.1 %collective-permute-start = (f32[8,16,32,128]{3,2,0,1:T(8,128)S(1)}, f32[8,16,32,128]{3,2,0,1:T(8,128)S(1)}, u32[]{:S(2)}, u32[]{:S(2)}) collective-permute-start(f32[8,16,32,128]{3,2,0,1:T(8,128)S(1)} %fusion.18), channel_id=1, source_target_pairs={{0,1},{1,0},{2,3},{3,2},{4,5},{5,4},{6,7},{7,6},{8,9},{9,8},{10,11... | collective-permute-start | bytes 6291464 | tf_op jit(solution)/shard_map/ppermute | solution.py:102
  204.8 47.6 %collective-permute-start.1 = (f32[8,16,32,128]{3,2,0,1:T(8,128)S(1)}, f32[8,16,32,128]{3,2,0,1:T(8,128)S(1)}, u32[]{:S(2)}, u32[]{:S(2)}) collective-permute-start(f32[8,16,32,128]{3,2,0,1:T(8,128)S(1)} %add.159), channel_id=1, source_target_pairs={{0,2},{1,3},{2,0},{3,1},{4,6},{5,7},{6,4},{7,5},{8,10},{9,11},{10,... | collective-permute-start | bytes 6291464 | tf_op jit(solution)/shard_map/ppermute | solution.py:102
  252.9 45.2 %collective-permute-start.2 = (f32[8,16,32,128]{3,2,0,1:T(8,128)S(1)}, f32[8,16,32,128]{3,2,0,1:T(8,128)S(1)}, u32[]{:S(2)}, u32[]{:S(2)}) collective-permute-start(f32[8,16,32,128]{3,2,0,1:T(8,128)S(1)} %add.160), channel_id=1, source_target_pairs={{0,4},{1,5},{2,6},{3,7},{4,0},{5,1},{6,2},{7,3},{8,12},{9,13},{10,... | collective-permute-start | bytes 6291464 | tf_op jit(solution)/shard_map/ppermute | solution.py:102
  298.7 46.2 %collective-permute-start.3 = (f32[8,16,32,128]{3,2,0,1:T(8,128)S(1)}, f32[8,16,32,128]{3,2,0,1:T(8,128)}, u32[]{:S(2)}, u32[]{:S(2)}) collective-permute-start(f32[8,16,32,128]{3,2,0,1:T(8,128)S(1)} %add.161), channel_id=1, source_target_pairs={{0,8},{1,9},{2,10},{3,11},{4,12},{5,13},{6,14},{7,15},{8,0},{9,1},... | collective-permute-start | bytes 6291464 | tf_op jit(solution)/shard_map/ppermute | solution.py:102
  352.0 12.4 %all-to-all-start = ((f32[8,1,4096]{2,1,0:T(1,128)}), f32[8,1,4096]{2,1,0:T(1,128)S(1)}, u32[]{:S(2)}, u32[]{:S(2)}) async-start(f32[8,1,4096]{2,1,0:T(1,128)} %reshape.192), calls=%async_computation | async-start | bytes 262144 | tf_op jit(solution)/shard_map/all_to_all | solution.py:109
  366.8 14.8 %copy-start.1 = (bf16[64,32,768]{2,1,0:T(8,128)(2,1)S(1)}, bf16[64,32,768]{2,1,0:T(8,128)(2,1)}, u32[]{:S(2)}) copy-start(bf16[64,32,768]{2,1,0:T(8,128)(2,1)} %param.11) | copy-start | bytes 9437188
Sparse Core Ops, SparseCore 0:
  43.0 28.5 all-gather.2
